TPU v7x, 32 devices: a whole 2x2x4 slice. The times are simulated.
32 devices in a mesh: lon: 2 (over core), lat: 4 (over y, x), mem: 4 (over z).
Axes of the slice: x: 2, y: 2, z: 4, core: 2. Of those that a mesh axis runs over, the one named last changes fastest.
Arguments:
- ensemble: bfloat16 [80, 4, 4, 128, 512], P('mem', None, None, 'lon', 'lat'), may hold values from -6 to 6
- huber: float32 [4, 4, 128, 512], P(None, None, 'lon', 'lat'), may hold values from 0.1 to 1
- innovation: float32 [4, 4, 128, 512], P(None, None, 'lon', 'lat'), may hold values from -6 to 6
- sea_mask: int32 [32, 128], P('lon', 'lat'), may hold values 0 or 1
Outputs:
- control: float32 [80, 4, 32, 128], P('mem', None, 'lon', 'lat')
- gradient: float32 [80, 4, 32, 128], P('mem', None, 'lon', 'lat')
All inputs are finite; a program needn't handle non-finite values. No bound on the sum of `sea_mask` on one device may be relied on, other than what follows from the above.
Results may differ from a plain program's by a relative error of at most 0.013.
Values may be sent and summed in bfloat16 or wider, within the bound.
No kernel may reach another device: no remote copies, remote signals or barrier semaphores. Data moves between devices by JAX's collectives and lax.ppermute only.
A program may use at most 128 MiB of HBM per device.

v0:
```python
import math
import jax
import jax.numpy as jnp
from jax import lax
from jax.sharding import PartitionSpec as P

MEMBERS = 80
RATIO = 4
DSTEPS = 4
ITERS = 3
diffusion_rate = 0.2


def extended(cells, sides, width):
    for axis, dim in sides:
        count = lax.axis_size(axis)
        ends = count - 1
        head = lax.slice_in_dim(cells, 0, width, axis=dim)
        tail = lax.slice_in_dim(cells, cells.shape[dim] - width, cells.shape[dim], axis=dim)
        cells = jnp.concatenate(
            [
                lax.ppermute(tail, axis, [(i, (i + 1) % count) for i in range(ends)]),
                cells,
                lax.ppermute(head, axis, [((i + 1) % count, i) for i in range(ends)]),
            ],
            axis=dim,
        )
    return cells


def hat_table(rows, cols, row_shift, col_shift):
    fine_pos = (jnp.arange(rows, dtype=jnp.float32) - row_shift + 0.5) / RATIO - 0.5
    coarse_pos = jnp.arange(cols, dtype=jnp.float32) - col_shift
    return jnp.maximum(0.0, 1.0 - jnp.abs(coarse_pos[None, :] - fine_pos[:, None]))


def smooth_once(padded):
    inner = padded[:, :, 1:-1, 1:-1]
    beside = (
        padded[:, :, 2:, 1:-1]
        + padded[:, :, :-2, 1:-1]
        + padded[:, :, 1:-1, 2:]
        + padded[:, :, 1:-1, :-2]
    )
    return inner + diffusion_rate * (beside - 4.0 * inner)


def inside_cells(count, width, position, devices):
    first = position * count - width
    where = first + jnp.arange(count + 2 * width, dtype=jnp.int32)
    whole = count * devices
    return ((where >= 0) & (where < whole)).astype(jnp.float32)


def smooth_deep(field, width):
    padded = extended(field, (("lon", 2), ("lat", 3)), width)
    rows_in = inside_cells(field.shape[2], width, lax.axis_index("lon"), lax.axis_size("lon"))
    cols_in = inside_cells(field.shape[3], width, lax.axis_index("lat"), lax.axis_size("lat"))
    for step in range(DSTEPS):
        padded = smooth_once(padded)
        trim = step + 1
        row_keep = rows_in[trim : rows_in.shape[0] - trim]
        col_keep = cols_in[trim : cols_in.shape[0] - trim]
        padded = padded * row_keep[:, None] * col_keep[None, :]
    return padded


def local(ensemble, huber, innovation, sea_mask):
    scale = 1.0 / math.sqrt(MEMBERS - 1)
    keep = sea_mask.astype(jnp.float32)
    cells_x, cells_y = sea_mask.shape
    fine_cols, fine_rows = (ensemble.shape[3], ensemble.shape[4])
    forward_x = hat_table(fine_cols, cells_x + 2, 0, 1)
    forward_y = hat_table(fine_rows, cells_y + 2, 0, 1)
    back_x = hat_table(fine_cols + 4, cells_x, 2, 0)
    back_y = hat_table(fine_rows + 4, cells_y, 2, 0)

    def adjoint(misfit):
        spread = (
            jnp.einsum("mvlxy,vlxy->mlxy", ensemble, misfit, preferred_element_type=jnp.float32)
            * scale
        )
        padded = extended(spread, (("lon", 2), ("lat", 3)), 2)
        back = jnp.einsum(
            "xc,mlxy,yd->mlcd", back_x, padded, back_y, precision=lax.Precision.HIGHEST
        )
        back = smooth_deep(back, DSTEPS)
        return keep * back

    misfit_start = (huber * innovation).astype(jnp.bfloat16)
    gradient = -adjoint(misfit_start)
    control = jnp.zeros_like(gradient)
    for step in range(ITERS):
        shaped = keep * gradient
        hessian_padded = smooth_deep(shaped, DSTEPS + 1)
        fine = jnp.einsum(
            "xc,mlcd,yd->mlxy",
            forward_x,
            hessian_padded,
            forward_y,
            precision=lax.Precision.HIGHEST,
        ).astype(jnp.bfloat16)
        partial_sum = jnp.einsum(
            "mvlxy,mlxy->vlxy", ensemble, fine, preferred_element_type=jnp.float32
        )
        total = lax.psum(partial_sum, "mem")
        hessian_misfit = (huber * (total * scale)).astype(jnp.bfloat16)
        image = gradient + adjoint(hessian_misfit)
        squares, curvature = lax.psum(
            (jnp.sum(gradient * gradient), jnp.sum(gradient * image)), ("lon", "lat", "mem")
        )
        alpha = squares / curvature
        control = control - alpha * gradient
        gradient = gradient - alpha * image
    return (control, gradient)


def solution(mesh):
    placed = (
        P("mem", None, None, "lon", "lat"),
        P(None, None, "lon", "lat"),
        P(None, None, "lon", "lat"),
        P("lon", "lat"),
    )
    return jax.shard_map(
        local,
        mesh=mesh,
        in_specs=placed,
        out_specs=(P("mem", None, "lon", "lat"), P("mem", None, "lon", "lat")),
        check_vma=False,
    )
```

profile of v0, /device:TPU:0, one launch (start us, length us, event | category | flops | bytes accessed | tf_op | source)
XLA Modules:
  0.0 666.2 jit_solution(17996090135539417670)
XLA Ops:
  8.5 4.2 fusion.3
  21.2 4.0 fusion.330
  31.3 5.4 collective-permute-start.2
  36.8 3.6 copy.99
  40.5 11.1 %fusion.7 = f32[20,4,132,16]{2,3,1,0:T(8,128)S(1)} fusion(f32[20,4,68,2]{2,3,1,0:T(2,128)S(1)} %copy.100, f32[20,4,68,128]{2,3,1,0:T(8,128)} %copy.99, f32[20,4,68,2]{2,3,1,0:T(2,128)S(1)} %copy.98, f32[68]{0:T(128)S(1)} %multiply_add_fusion.3), kind=kOutput, calls=%fused_computation.14 | convolution fusion | flops 139311872 | bytes 3548432 | tf_op jit(solution)/shard_map/xc,mlxy,yd->mlcd/dot_general | solution.py:84
  59.0 4.5 collective-permute-start.6
  67.9 4.4 collective-permute-done.7
  87.9 4.2 collective-permute-start.10
  97.8 4.5 collective-permute-done.11
  102.4 2.6 copy.108
  117.4 37.6 %all-reduce.7.cloned.1.call-done = f32[4,4,64,128]{3,2,1,0:T(8,128)} async-done(((f32[4,4,64,128]{3,2,1,0:T(8,128)}), f32[4,4,64,128]{3,2,1,0:T(8,128)}) %all-reduce.7.cloned.1.call-update) | async-done | bytes 524304 | tf_op jit(solution)/shard_map/psum | solution.py:106
  156.1 4.2 fusion.4
  167.7 4.0 fusion.329
  174.1 4.0 collective-permute-start.14
  178.1 3.0 copy.216
  182.6 3.6 copy.114
  188.7 11.1 %fusion.13 = f32[20,4,132,16]{2,3,1,0:T(8,128)S(1)} fusion(f32[20,4,68,2]{2,3,1,0:T(2,128)S(1)} %copy.115, f32[20,4,68,128]{2,3,1,0:T(8,128)} %copy.114, f32[20,4,68,2]{2,3,1,0:T(2,128)S(1)} %copy.113, f32[68]{0:T(128)} %copy-done.22), kind=kOutput, calls=%fused_computation.20 | convolution fusion | flops 139311872 | bytes 3548432 | tf_op jit(solution)/shard_map/xc,mlxy,yd->mlcd/dot_general | solution.py:84
  208.1 4.1 collective-permute-start.18
  216.8 5.2 collective-permute-done.19
  229.8 39.9 %all-reduce.2 = (f32[]{:T(128)}, f32[]{:T(128)}) all-reduce(f32[]{:T(128)} %get-tuple-element.7, f32[]{:T(128)} %get-tuple-element.6), channel_id=1, replica_groups=mesh['lon'=2,'lat'=4,'mem'=4] {'lon','lat','mem'}, use_global_device_ids=true, to_apply=%region_1.0 | all-reduce | flops 2 | bytes 16 | tf_op jit(solution)/shard_map/psum | solution.py:109
  278.7 2.6 copy.120
  281.3 4.9 collective-permute-start.22
  292.0 4.9 collective-permute-done.23
  296.9 2.6 copy.123
  311.9 37.1 %all-reduce.9.cloned.1.call-done = f32[4,4,64,128]{3,2,1,0:T(8,128)} async-done(((f32[4,4,64,128]{3,2,1,0:T(8,128)}), f32[4,4,64,128]{3,2,1,0:T(8,128)}) %all-reduce.9.cloned.1.call-update) | async-done | bytes 524304 | tf_op jit(solution)/shard_map/psum | solution.py:106
  350.1 4.2 fusion.5
  361.7 4.0 fusion.328
  368.0 4.0 collective-permute-start.26
  372.1 3.0 copy.218
  376.4 3.6 copy.129
  382.7 11.1 %fusion.19 = f32[20,4,132,16]{2,3,1,0:T(8,128)S(1)} fusion(f32[20,4,68,2]{2,3,1,0:T(2,128)S(1)} %copy.130, f32[20,4,68,128]{2,3,1,0:T(8,128)} %copy.129, f32[20,4,68,2]{2,3,1,0:T(2,128)S(1)} %copy.128, f32[68]{0:T(128)} %copy-done.22), kind=kOutput, calls=%fused_computation.26 | convolution fusion | flops 139311872 | bytes 3548432 | tf_op jit(solution)/shard_map/xc,mlxy,yd->mlcd/dot_general | solution.py:84
  402.0 4.0 collective-permute-start.30
  410.6 5.1 collective-permute-done.31
  423.6 39.5 %all-reduce.1 = (f32[]{:T(128)}, f32[]{:T(128)}) all-reduce(f32[]{:T(128)} %get-tuple-element.5, f32[]{:T(128)} %get-tuple-element.4), channel_id=1, replica_groups=mesh['lon'=2,'lat'=4,'mem'=4] {'lon','lat','mem'}, use_global_device_ids=true, to_apply=%region_6.0 | all-reduce | flops 2 | bytes 16 | tf_op jit(solution)/shard_map/psum | solution.py:109
  472.2 2.6 copy.135
  474.7 4.9 collective-permute-start.34
  485.4 5.0 collective-permute-done.35
  490.4 2.6 copy.138
  505.1 37.3 %all-reduce.11.cloned.1.call-done = f32[4,4,64,128]{3,2,1,0:T(8,128)} async-done(((f32[4,4,64,128]{3,2,1,0:T(8,128)}), f32[4,4,64,128]{3,2,1,0:T(8,128)}) %all-reduce.11.cloned.1.call-update) | async-done | bytes 524304 | tf_op jit(solution)/shard_map/psum | solution.py:106
  543.6 4.2 fusion.6
  555.3 4.0 fusion.327
  561.7 4.0 collective-permute-start.38
  565.7 3.0 copy.220
  570.0 3.6 copy.144
  576.3 11.1 %fusion.25 = f32[20,4,132,16]{2,3,1,0:T(8,128)S(1)} fusion(f32[20,4,68,2]{2,3,1,0:T(2,128)S(1)} %copy.145, f32[20,4,68,128]{2,3,1,0:T(8,128)} %copy.144, f32[20,4,68,2]{2,3,1,0:T(2,128)S(1)} %copy.143, f32[68]{0:T(128)} %copy-done.22), kind=kOutput, calls=%fused_computation.32 | convolution fusion | flops 139311872 | bytes 3548432 | tf_op jit(solution)/shard_map/xc,mlxy,yd->mlcd/dot_general | solution.py:84
  595.7 4.0 collective-permute-start.42
  604.3 5.2 collective-permute-done.43
  617.3 39.5 %all-reduce = (f32[]{:T(128)}, f32[]{:T(128)}) all-reduce(f32[]{:T(128)} %get-tuple-element.3, f32[]{:T(128)} %get-tuple-element.2), channel_id=1, replica_groups=mesh['lon'=2,'lat'=4,'mem'=4] {'lon','lat','mem'}, use_global_device_ids=true, to_apply=%region_11.0 | all-reduce | flops 2 | bytes 16 | tf_op jit(solution)/shard_map/psum | solution.py:109
  (361 shorter events, 219.1 us)
Async XLA Ops:
  7.2 147.8 %all-reduce.7.cloned.1.call-start = ((), (), s32[]{:S(2)}) async-start(), calls=%async_computation | async-start | bytes 1048576 | tf_op jit(solution)/shard_map/psum | solution.py:106
  15.0 3.8 collective-permute-start
  17.4 3.2 collective-permute-start.1
  18.8 93.6 %copy-start.23 = (f32[18]{0:T(128)}, f32[18]{0:T(128)S(1)}, u32[]{:S(2)}) copy-start(f32[18]{0:T(128)S(1)} %iota_add_fusion) | copy-start | bytes 220
  27.6 12.7 %collective-permute-start.3 = (f32[20,4,68,2]{2,1,3,0:T(4,128)S(1)}, f32[20,4,68,2]{2,1,3,0:T(4,128)S(1)}, u32[]{:S(2)}, u32[]{:S(2)}) collective-permute-start(f32[20,4,68,2]{2,1,3,0:T(4,128)S(1)} %copy.214), channel_id=1, source_target_pairs={{4,0},{8,4},{12,8},{5,1},{9,5},{13,9},{6,2},{10,6},{14,10},{7,3},{... | collective-permute-start | bytes 130568 | tf_op jit(solution)/shard_map/ppermute | solution.py:24
  31.3 9.1 %collective-permute-start.2 = (f32[20,4,68,2]{2,1,3,0:T(4,128)S(1)}, f32[20,4,68,2]{2,1,3,0:T(4,128)S(1)}, u32[]{:S(2)}, u32[]{:S(2)}) collective-permute-start(f32[20,4,68,2]{2,1,3,0:T(4,128)S(1)} %copy.213), channel_id=1, source_target_pairs={{0,4},{4,8},{8,12},{1,5},{5,9},{9,13},{2,6},{6,10},{10,14},{3,7},{... | collective-permute-start | bytes 130568 | tf_op jit(solution)/shard_map/ppermute | solution.py:22
  52.9 3.1 collective-permute-start.4
  54.7 3.3 collective-permute-start.5
  59.0 8.3 %collective-permute-start.6 = (f32[20,4,24,4]{2,3,1,0:T(4,128)S(1)}, f32[20,4,24,4]{2,3,1,0:T(4,128)S(1)}, u32[]{:S(2)}, u32[]{:S(2)}) collective-permute-start(f32[20,4,24,4]{2,3,1,0:T(4,128)S(1)} %copy.101), channel_id=1, source_target_pairs={{0,4},{4,8},{8,12},{1,5},{5,9},{9,13},{2,6},{6,10},{10,14},{3,7},{... | collective-permute-start | bytes 92168 | tf_op jit(solution)/shard_map/ppermute | solution.py:22
  64.2 8.1 %collective-permute-start.7 = (f32[20,4,24,4]{2,3,1,0:T(4,128)S(1)}, f32[20,4,24,4]{2,3,1,0:T(4,128)}, u32[]{:S(2)}, u32[]{:S(2)}) collective-permute-start(f32[20,4,24,4]{2,3,1,0:T(4,128)S(1)} %copy.102), channel_id=1, source_target_pairs={{4,0},{8,4},{12,8},{5,1},{9,5},{13,9},{6,2},{10,6},{14,10},{7,3},{... | collective-permute-start | bytes 92168 | tf_op jit(solution)/shard_map/ppermute | solution.py:24
  78.6 2.6 collective-permute-start.8
  80.0 3.5 collective-permute-start.9
  87.9 8.4 %collective-permute-start.10 = (f32[20,4,26,5]{2,1,3,0:T(4,128)}, f32[20,4,26,5]{2,1,3,0:T(4,128)}, u32[]{:S(2)}, u32[]{:S(2)}) collective-permute-start(f32[20,4,26,5]{2,1,3,0:T(4,128)} %copy.105), channel_id=1, source_target_pairs={{0,4},{4,8},{8,12},{1,5},{5,9},{9,13},{2,6},{6,10},{10,14},{3,7},{... | collective-permute-start | bytes 124808 | tf_op jit(solution)/shard_map/ppermute | solution.py:22
  93.3 9.0 %collective-permute-start.11 = (f32[20,4,26,5]{2,1,3,0:T(4,128)}, f32[20,4,26,5]{2,1,3,0:T(4,128)}, u32[]{:S(2)}, u32[]{:S(2)}) collective-permute-start(f32[20,4,26,5]{2,1,3,0:T(4,128)} %copy.106), channel_id=1, source_target_pairs={{4,0},{8,4},{12,8},{5,1},{9,5},{13,9},{6,2},{10,6},{14,10},{7,3},{... | collective-permute-start | bytes 124808 | tf_op jit(solution)/shard_map/ppermute | solution.py:24
  117.0 232.0 %all-reduce.9.cloned.1.call-start = ((), (), s32[]{:S(2)}) async-start(), calls=%async_computation.1 | async-start | bytes 1048576 | tf_op jit(solution)/shard_map/psum | solution.py:106
  162.6 2.6 collective-permute-start.12
  163.9 3.2 collective-permute-start.13
  174.1 12.1 %collective-permute-start.14 = (f32[20,4,68,2]{2,1,3,0:T(4,128)S(1)}, f32[20,4,68,2]{2,1,3,0:T(4,128)}, u32[]{:S(2)}, u32[]{:S(2)}) collective-permute-start(f32[20,4,68,2]{2,1,3,0:T(4,128)S(1)} %copy.215), channel_id=1, source_target_pairs={{0,4},{4,8},{8,12},{1,5},{5,9},{9,13},{2,6},{6,10},{10,14},{3,7},{... | collective-permute-start | bytes 130568 | tf_op jit(solution)/shard_map/ppermute | solution.py:22
  181.1 6.6 collective-permute-start.15
  201.1 2.6 collective-permute-start.16
  202.4 3.3 collective-permute-start.17
  208.1 8.2 %collective-permute-start.18 = (f32[20,4,24,4]{2,3,1,0:T(4,128)}, f32[20,4,24,4]{2,3,1,0:T(4,128)S(1)}, u32[]{:S(2)}, u32[]{:S(2)}) collective-permute-start(f32[20,4,24,4]{2,3,1,0:T(4,128)} %copy.116), channel_id=1, source_target_pairs={{0,4},{4,8},{8,12},{1,5},{5,9},{9,13},{2,6},{6,10},{10,14},{3,7},{... | collective-permute-start | bytes 92168 | tf_op jit(solution)/shard_map/ppermute | solution.py:22
  212.8 9.2 %collective-permute-start.19 = (f32[20,4,24,4]{2,3,1,0:T(4,128)S(1)}, f32[20,4,24,4]{2,3,1,0:T(4,128)}, u32[]{:S(2)}, u32[]{:S(2)}) collective-permute-start(f32[20,4,24,4]{2,3,1,0:T(4,128)S(1)} %copy.117), channel_id=1, source_target_pairs={{4,0},{8,4},{12,8},{5,1},{9,5},{13,9},{6,2},{10,6},{14,10},{7,3},{... | collective-permute-start | bytes 92168 | tf_op jit(solution)/shard_map/ppermute | solution.py:24
  272.1 2.6 collective-permute-start.20
  273.4 3.5 collective-permute-start.21
  281.3 9.1 %collective-permute-start.22 = (f32[20,4,26,5]{2,1,3,0:T(4,128)}, f32[20,4,26,5]{2,1,3,0:T(4,128)}, u32[]{:S(2)}, u32[]{:S(2)}) collective-permute-start(f32[20,4,26,5]{2,1,3,0:T(4,128)} %copy.120), channel_id=1, source_target_pairs={{0,4},{4,8},{8,12},{1,5},{5,9},{9,13},{2,6},{6,10},{10,14},{3,7},{... | collective-permute-start | bytes 124808 | tf_op jit(solution)/shard_map/ppermute | solution.py:22
  287.5 9.5 %collective-permute-start.23 = (f32[20,4,26,5]{2,1,3,0:T(4,128)}, f32[20,4,26,5]{2,1,3,0:T(4,128)}, u32[]{:S(2)}, u32[]{:S(2)}) collective-permute-start(f32[20,4,26,5]{2,1,3,0:T(4,128)} %copy.121), channel_id=1, source_target_pairs={{4,0},{8,4},{12,8},{5,1},{9,5},{13,9},{6,2},{10,6},{14,10},{7,3},{... | collective-permute-start | bytes 124808 | tf_op jit(solution)/shard_map/ppermute | solution.py:24
  311.6 230.8 %all-reduce.11.cloned.1.call-start = ((), (), s32[]{:S(2)}) async-start(), calls=%async_computation.2 | async-start | bytes 1048576 | tf_op jit(solution)/shard_map/psum | solution.py:106
  356.6 2.6 collective-permute-start.24
  357.9 3.2 collective-permute-start.25
  368.0 11.9 %collective-permute-start.26 = (f32[20,4,68,2]{2,1,3,0:T(4,128)S(1)}, f32[20,4,68,2]{2,1,3,0:T(4,128)}, u32[]{:S(2)}, u32[]{:S(2)}) collective-permute-start(f32[20,4,68,2]{2,1,3,0:T(4,128)S(1)} %copy.217), channel_id=1, source_target_pairs={{0,4},{4,8},{8,12},{1,5},{5,9},{9,13},{2,6},{6,10},{10,14},{3,7},{... | collective-permute-start | bytes 130568 | tf_op jit(solution)/shard_map/ppermute | solution.py:22
  375.1 6.6 collective-permute-start.27
  395.0 2.6 collective-permute-start.28
  396.4 3.3 collective-permute-start.29
  402.0 8.0 %collective-permute-start.30 = (f32[20,4,24,4]{2,3,1,0:T(4,128)}, f32[20,4,24,4]{2,3,1,0:T(4,128)S(1)}, u32[]{:S(2)}, u32[]{:S(2)}) collective-permute-start(f32[20,4,24,4]{2,3,1,0:T(4,128)} %copy.131), channel_id=1, source_target_pairs={{0,4},{4,8},{8,12},{1,5},{5,9},{9,13},{2,6},{6,10},{10,14},{3,7},{... | collective-permute-start | bytes 92168 | tf_op jit(solution)/shard_map/ppermute | solution.py:22
  406.6 9.2 %collective-permute-start.31 = (f32[20,4,24,4]{2,3,1,0:T(4,128)S(1)}, f32[20,4,24,4]{2,3,1,0:T(4,128)}, u32[]{:S(2)}, u32[]{:S(2)}) collective-permute-start(f32[20,4,24,4]{2,3,1,0:T(4,128)S(1)} %copy.132), channel_id=1, source_target_pairs={{4,0},{8,4},{12,8},{5,1},{9,5},{13,9},{6,2},{10,6},{14,10},{7,3},{... | collective-permute-start | bytes 92168 | tf_op jit(solution)/shard_map/ppermute | solution.py:24
  465.5 2.6 collective-permute-start.32
  466.8 3.5 collective-permute-start.33
  474.7 9.1 %collective-permute-start.34 = (f32[20,4,26,5]{2,1,3,0:T(4,128)}, f32[20,4,26,5]{2,1,3,0:T(4,128)}, u32[]{:S(2)}, u32[]{:S(2)}) collective-permute-start(f32[20,4,26,5]{2,1,3,0:T(4,128)} %copy.135), channel_id=1, source_target_pairs={{0,4},{4,8},{8,12},{1,5},{5,9},{9,13},{2,6},{6,10},{10,14},{3,7},{... | collective-permute-start | bytes 124808 | tf_op jit(solution)/shard_map/ppermute | solution.py:22
  480.9 9.5 %collective-permute-start.35 = (f32[20,4,26,5]{2,1,3,0:T(4,128)}, f32[20,4,26,5]{2,1,3,0:T(4,128)}, u32[]{:S(2)}, u32[]{:S(2)}) collective-permute-start(f32[20,4,26,5]{2,1,3,0:T(4,128)} %copy.136), channel_id=1, source_target_pairs={{4,0},{8,4},{12,8},{5,1},{9,5},{13,9},{6,2},{10,6},{14,10},{7,3},{... | collective-permute-start | bytes 124808 | tf_op jit(solution)/shard_map/ppermute | solution.py:24
  550.2 2.6 collective-permute-start.36
  551.5 3.2 collective-permute-start.37
  561.7 12.0 %collective-permute-start.38 = (f32[20,4,68,2]{2,1,3,0:T(4,128)S(1)}, f32[20,4,68,2]{2,1,3,0:T(4,128)}, u32[]{:S(2)}, u32[]{:S(2)}) collective-permute-start(f32[20,4,68,2]{2,1,3,0:T(4,128)S(1)} %copy.219), channel_id=1, source_target_pairs={{0,4},{4,8},{8,12},{1,5},{5,9},{9,13},{2,6},{6,10},{10,14},{3,7},{... | collective-permute-start | bytes 130568 | tf_op jit(solution)/shard_map/ppermute | solution.py:22
  568.8 6.6 collective-permute-start.39
  588.7 2.6 collective-permute-start.40
  590.0 3.3 collective-permute-start.41
  595.7 8.0 %collective-permute-start.42 = (f32[20,4,24,4]{2,3,1,0:T(4,128)}, f32[20,4,24,4]{2,3,1,0:T(4,128)S(1)}, u32[]{:S(2)}, u32[]{:S(2)}) collective-permute-start(f32[20,4,24,4]{2,3,1,0:T(4,128)} %copy.146), channel_id=1, source_target_pairs={{0,4},{4,8},{8,12},{1,5},{5,9},{9,13},{2,6},{6,10},{10,14},{3,7},{... | collective-permute-start | bytes 92168 | tf_op jit(solution)/shard_map/ppermute | solution.py:22
  600.2 9.2 %collective-permute-start.43 = (f32[20,4,24,4]{2,3,1,0:T(4,128)S(1)}, f32[20,4,24,4]{2,3,1,0:T(4,128)}, u32[]{:S(2)}, u32[]{:S(2)}) collective-permute-start(f32[20,4,24,4]{2,3,1,0:T(4,128)S(1)} %copy.147), channel_id=1, source_target_pairs={{4,0},{8,4},{12,8},{5,1},{9,5},{13,9},{6,2},{10,6},{14,10},{7,3},{... | collective-permute-start | bytes 92168 | tf_op jit(solution)/shard_map/ppermute | solution.py:24
  (64 other events, 707.7 us)
Sparse Core Ops, SparseCore 0:
  117.1 37.8 all-reduce.6
  311.8 37.1 all-reduce.8
  505.3 37.1 all-reduce.10
where the time goes:
time: 674 us; the launch traced here: 666 us
  waiting for transfers between devices  182 us (27%)
  blocking collectives  119 us (18%)
  local copies, waits for them, and re-layouts  113 us (17%)
  starting transfers between devices  94.1 us (14%)
  other arithmetic  76.6 us (11%)
  matrix products  61.5 us (9%)
  between operations  20 us (3%)
    psum x3, blocking collectives, local(): lax.psum((jnp.sum(gradient * gradient), jnp.sum(gradient * image)), ('lon...  119 us
    psum x3, waiting for transfers between devices, local(): total = lax.psum(partial_sum, 'mem')  112 us
    ppermute x22, starting transfers between devices, extended(): lax.ppermute(tail, axis, [(i, (i + 1) % count) for i in range(ends)])  63.9 us
    ppermute x22, waiting for transfers between devices, extended(): lax.ppermute(head, axis, [((i + 1) % count, i) for i in range(ends)])  58.4 us
    dot_general x8, matrix products, adjoint(): jnp.einsum('xc,mlxy,yd->mlcd', back_x, padded, back_y, precision=lax.Prec...  49.3 us
    slice x29, local copies, waits for them, and re-layouts, extended(): lax.slice_in_dim(cells, cells.shape[dim] - width, cells.shape[dim], axis=...  34.3 us
    unnamed x142, local copies, waits for them, and re-layouts  31.1 us
    ppermute x22, starting transfers between devices, extended(): lax.ppermute(head, axis, [((i + 1) % count, i) for i in range(ends)])  29.5 us
  transfers between devices with their start and end apart: 47, of which 31 were waited for; matrix products, arithmetic and copies ran while one was open for 6% of the time, Pallas kernels for 0%

commit v1 on v0

--- a/solution.py
+++ b/solution.py
@@ -103,7 +103,8 @@
         partial_sum = jnp.einsum(
             "mvlxy,mlxy->vlxy", ensemble, fine, preferred_element_type=jnp.float32
         )
-        total = lax.psum(partial_sum, "mem")
+        parts = lax.all_gather(partial_sum, "mem", axis=0, tiled=False)
+        total = parts.sum(axis=0)
         hessian_misfit = (huber * (total * scale)).astype(jnp.bfloat16)
         image = gradient + adjoint(hessian_misfit)
         squares, curvature = lax.psum(

time: 674 us -> 696 us (1.033)
  waiting for transfers between devices: 182 us -> 205 us
    all_gather x0 -> x3, waiting for transfers between devices: none -> 134 us  [local(): parts = lax.all_gather(partial_sum, 'mem', axis=0, tiled=False)]
    psum x3 -> x0, waiting for transfers between devices: 112 us -> none  [local(): total = lax.psum(partial_sum, 'mem')]
  transfers between devices with their start and end apart: 47 -> 47, of which waited for: 31 -> 32; matrix products, arithmetic and copies ran while one was open for 6% -> 6% of each run, Pallas kernels for 0% -> 0%
where the time goes in v1:
time: 696 us; the launch traced here: 688 us
  waiting for transfers between devices  205 us (29%)
  blocking collectives  115 us (17%)
  local copies, waits for them, and re-layouts  113 us (16%)
  starting transfers between devices  94.2 us (14%)
  other arithmetic  78.9 us (11%)
  matrix products  61.5 us (9%)
  between operations  20 us (3%)
    all_gather x3, waiting for transfers between devices, local(): parts = lax.all_gather(partial_sum, 'mem', axis=0, tiled=False)  134 us
    psum x3, blocking collectives, local(): lax.psum((jnp.sum(gradient * gradient), jnp.sum(gradient * image)), ('lon...  115 us
    ppermute x22, starting transfers between devices, extended(): lax.ppermute(tail, axis, [(i, (i + 1) % count) for i in range(ends)])  63.2 us
    ppermute x22, waiting for transfers between devices, extended(): lax.ppermute(head, axis, [((i + 1) % count, i) for i in range(ends)])  60.2 us
    dot_general x8, matrix products, adjoint(): jnp.einsum('xc,mlxy,yd->mlcd', back_x, padded, back_y, precision=lax.Prec...  49.3 us
    slice x29, local copies, waits for them, and re-layouts, extended(): lax.slice_in_dim(cells, cells.shape[dim] - width, cells.shape[dim], axis=...  34.3 us
    unnamed x142, local copies, waits for them, and re-layouts  31.1 us
    ppermute x22, starting transfers between devices, extended(): lax.ppermute(head, axis, [((i + 1) % count, i) for i in range(ends)])  30 us
  transfers between devices with their start and end apart: 47, of which 32 were waited for; matrix products, arithmetic and copies ran while one was open for 6% of the time, Pallas kernels for 0%

profile of v1, /device:TPU:0, one launch (start us, length us, event | category | flops | bytes accessed | tf_op | source)
XLA Modules:
  0.0 688.4 jit_solution(11107706044351017210)
XLA Ops:
  8.5 4.2 fusion.3
  21.2 4.0 fusion.330
  27.6 4.2 collective-permute-start.2
  36.1 3.6 copy.109
  40.7 11.1 %fusion.7 = f32[20,4,132,16]{2,3,1,0:T(8,128)S(1)} fusion(f32[20,4,68,2]{2,3,1,0:T(2,128)S(1)} %copy.110, f32[20,4,68,128]{2,3,1,0:T(8,128)} %copy.109, f32[20,4,68,2]{2,3,1,0:T(2,128)S(1)} %copy.108, f32[68]{0:T(128)S(1)} %multiply_add_fusion.3), kind=kOutput, calls=%fused_computation.14 | convolution fusion | flops 139311872 | bytes 3548432 | tf_op jit(solution)/shard_map/xc,mlxy,yd->mlcd/dot_general | solution.py:84
  58.7 4.3 collective-permute-start.6
  67.3 5.6 collective-permute-done.7
  88.5 4.2 collective-permute-start.10
  98.5 4.5 collective-permute-done.11
  103.0 2.6 copy.118
  118.0 44.7 %all-gather.7.cloned.1.call-done = f32[16,4,64,128]{3,2,1,0:T(8,128)} async-done(((f32[4,4,64,128]{3,2,1,0:T(8,128)}), f32[16,4,64,128]{3,2,1,0:T(8,128)}) %all-gather.7.cloned.1.call-update) | async-done | bytes 2097168 | tf_op jit(solution)/shard_map/all_gather | solution.py:106
  164.6 4.2 fusion.4
  176.5 4.0 fusion.329
  182.9 4.0 collective-permute-start.14
  186.9 3.0 copy.226
  191.4 3.6 copy.124
  197.5 11.1 %fusion.13 = f32[20,4,132,16]{2,3,1,0:T(8,128)S(1)} fusion(f32[20,4,68,2]{2,3,1,0:T(2,128)S(1)} %copy.125, f32[20,4,68,128]{2,3,1,0:T(8,128)} %copy.124, f32[20,4,68,2]{2,3,1,0:T(2,128)S(1)} %copy.123, f32[68]{0:T(128)} %copy-done.22), kind=kOutput, calls=%fused_computation.20 | convolution fusion | flops 139311872 | bytes 3548432 | tf_op jit(solution)/shard_map/xc,mlxy,yd->mlcd/dot_general | solution.py:84
  216.9 4.1 collective-permute-start.18
  225.6 5.1 collective-permute-done.19
  238.6 38.5 %all-reduce.2 = (f32[]{:T(128)}, f32[]{:T(128)}) all-reduce(f32[]{:T(128)} %get-tuple-element.7, f32[]{:T(128)} %get-tuple-element.6), channel_id=1, replica_groups=mesh['lon'=2,'lat'=4,'mem'=4] {'lon','lat','mem'}, use_global_device_ids=true, to_apply=%region_1.0 | all-reduce | flops 2 | bytes 16 | tf_op jit(solution)/shard_map/psum | solution.py:110
  286.1 2.6 copy.130
  288.7 4.9 collective-permute-start.22
  299.4 4.9 collective-permute-done.23
  304.3 2.6 copy.133
  319.5 44.3 %all-gather.9.cloned.1.call-done = f32[16,4,64,128]{3,2,1,0:T(8,128)} async-done(((f32[4,4,64,128]{3,2,1,0:T(8,128)}), f32[16,4,64,128]{3,2,1,0:T(8,128)}) %all-gather.9.cloned.1.call-update) | async-done | bytes 2097168 | tf_op jit(solution)/shard_map/all_gather | solution.py:106
  365.7 4.2 fusion.5
  377.5 4.0 fusion.328
  383.9 4.0 collective-permute-start.26
  387.9 3.0 copy.228
  392.4 3.6 copy.139
  398.5 11.1 %fusion.19 = f32[20,4,132,16]{2,3,1,0:T(8,128)S(1)} fusion(f32[20,4,68,2]{2,3,1,0:T(2,128)S(1)} %copy.140, f32[20,4,68,128]{2,3,1,0:T(8,128)} %copy.139, f32[20,4,68,2]{2,3,1,0:T(2,128)S(1)} %copy.138, f32[68]{0:T(128)} %copy-done.22), kind=kOutput, calls=%fused_computation.26 | convolution fusion | flops 139311872 | bytes 3548432 | tf_op jit(solution)/shard_map/xc,mlxy,yd->mlcd/dot_general | solution.py:84
  417.9 4.1 collective-permute-start.30
  426.7 5.2 collective-permute-done.31
  439.6 38.3 %all-reduce.1 = (f32[]{:T(128)}, f32[]{:T(128)}) all-reduce(f32[]{:T(128)} %get-tuple-element.5, f32[]{:T(128)} %get-tuple-element.4), channel_id=1, replica_groups=mesh['lon'=2,'lat'=4,'mem'=4] {'lon','lat','mem'}, use_global_device_ids=true, to_apply=%region_6.0 | all-reduce | flops 2 | bytes 16 | tf_op jit(solution)/shard_map/psum | solution.py:110
  487.0 2.6 copy.145
  489.6 4.9 collective-permute-start.34
  500.3 5.0 collective-permute-done.35
  505.3 2.6 copy.148
  520.0 44.7 %all-gather.11.cloned.1.call-done = f32[16,4,64,128]{3,2,1,0:T(8,128)} async-done(((f32[4,4,64,128]{3,2,1,0:T(8,128)}), f32[16,4,64,128]{3,2,1,0:T(8,128)}) %all-gather.11.cloned.1.call-update) | async-done | bytes 2097168 | tf_op jit(solution)/shard_map/all_gather | solution.py:106
  566.6 4.4 fusion.6
  578.6 4.0 fusion.327
  585.0 4.0 collective-permute-start.38
  589.0 3.0 copy.230
  593.3 3.6 copy.154
  599.6 11.1 %fusion.25 = f32[20,4,132,16]{2,3,1,0:T(8,128)S(1)} fusion(f32[20,4,68,2]{2,3,1,0:T(2,128)S(1)} %copy.155, f32[20,4,68,128]{2,3,1,0:T(8,128)} %copy.154, f32[20,4,68,2]{2,3,1,0:T(2,128)S(1)} %copy.153, f32[68]{0:T(128)} %copy-done.22), kind=kOutput, calls=%fused_computation.32 | convolution fusion | flops 139311872 | bytes 3548432 | tf_op jit(solution)/shard_map/xc,mlxy,yd->mlcd/dot_general | solution.py:84
  619.0 4.2 collective-permute-start.42
  627.6 5.2 collective-permute-done.43
  640.6 38.3 %all-reduce = (f32[]{:T(128)}, f32[]{:T(128)}) all-reduce(f32[]{:T(128)} %get-tuple-element.3, f32[]{:T(128)} %get-tuple-element.2), channel_id=1, replica_groups=mesh['lon'=2,'lat'=4,'mem'=4] {'lon','lat','mem'}, use_global_device_ids=true, to_apply=%region_11.0 | all-reduce | flops 2 | bytes 16 | tf_op jit(solution)/shard_map/psum | solution.py:110
  (364 shorter events, 223.0 us)
Async XLA Ops:
  7.2 155.6 %all-gather.7.cloned.1.call-start = ((), (), s32[]{:S(2)}) async-start(), calls=%async_computation | async-start | bytes 2621440 | tf_op jit(solution)/shard_map/all_gather | solution.py:106
  15.0 3.8 collective-permute-start
  17.4 3.2 collective-permute-start.1
  18.8 94.2 %copy-start.23 = (f32[18]{0:T(128)}, f32[18]{0:T(128)S(1)}, u32[]{:S(2)}) copy-start(f32[18]{0:T(128)S(1)} %iota_add_fusion) | copy-start | bytes 220
  27.6 12.1 %collective-permute-start.2 = (f32[20,4,68,2]{2,1,3,0:T(4,128)S(1)}, f32[20,4,68,2]{2,1,3,0:T(4,128)S(1)}, u32[]{:S(2)}, u32[]{:S(2)}) collective-permute-start(f32[20,4,68,2]{2,1,3,0:T(4,128)S(1)} %copy.223), channel_id=1, source_target_pairs={{0,4},{4,8},{8,12},{1,5},{5,9},{9,13},{2,6},{6,10},{10,14},{3,7},{... | collective-permute-start | bytes 130568 | tf_op jit(solution)/shard_map/ppermute | solution.py:22
  34.3 6.3 collective-permute-start.3
  53.0 2.6 collective-permute-start.4
  54.4 3.3 collective-permute-start.5
  58.7 8.1 %collective-permute-start.6 = (f32[20,4,24,4]{2,3,1,0:T(4,128)S(1)}, f32[20,4,24,4]{2,3,1,0:T(4,128)S(1)}, u32[]{:S(2)}, u32[]{:S(2)}) collective-permute-start(f32[20,4,24,4]{2,3,1,0:T(4,128)S(1)} %copy.111), channel_id=1, source_target_pairs={{0,4},{4,8},{8,12},{1,5},{5,9},{9,13},{2,6},{6,10},{10,14},{3,7},{... | collective-permute-start | bytes 92168 | tf_op jit(solution)/shard_map/ppermute | solution.py:22
  63.6 9.3 %collective-permute-start.7 = (f32[20,4,24,4]{2,3,1,0:T(4,128)S(1)}, f32[20,4,24,4]{2,3,1,0:T(4,128)}, u32[]{:S(2)}, u32[]{:S(2)}) collective-permute-start(f32[20,4,24,4]{2,3,1,0:T(4,128)S(1)} %copy.112), channel_id=1, source_target_pairs={{4,0},{8,4},{12,8},{5,1},{9,5},{13,9},{6,2},{10,6},{14,10},{7,3},{... | collective-permute-start | bytes 92168 | tf_op jit(solution)/shard_map/ppermute | solution.py:24
  79.3 2.6 collective-permute-start.8
  80.6 3.5 collective-permute-start.9
  88.5 8.4 %collective-permute-start.10 = (f32[20,4,26,5]{2,1,3,0:T(4,128)}, f32[20,4,26,5]{2,1,3,0:T(4,128)}, u32[]{:S(2)}, u32[]{:S(2)}) collective-permute-start(f32[20,4,26,5]{2,1,3,0:T(4,128)} %copy.115), channel_id=1, source_target_pairs={{0,4},{4,8},{8,12},{1,5},{5,9},{9,13},{2,6},{6,10},{10,14},{3,7},{... | collective-permute-start | bytes 124808 | tf_op jit(solution)/shard_map/ppermute | solution.py:22
  93.9 9.0 %collective-permute-start.11 = (f32[20,4,26,5]{2,1,3,0:T(4,128)}, f32[20,4,26,5]{2,1,3,0:T(4,128)}, u32[]{:S(2)}, u32[]{:S(2)}) collective-permute-start(f32[20,4,26,5]{2,1,3,0:T(4,128)} %copy.116), channel_id=1, source_target_pairs={{4,0},{8,4},{12,8},{5,1},{9,5},{13,9},{6,2},{10,6},{14,10},{7,3},{... | collective-permute-start | bytes 124808 | tf_op jit(solution)/shard_map/ppermute | solution.py:24
  117.6 246.2 %all-gather.9.cloned.1.call-start = ((), (), s32[]{:S(2)}) async-start(), calls=%async_computation.1 | async-start | bytes 2621440 | tf_op jit(solution)/shard_map/all_gather | solution.py:106
  171.1 2.9 collective-permute-start.12
  172.7 3.2 collective-permute-start.13
  182.9 12.1 %collective-permute-start.14 = (f32[20,4,68,2]{2,1,3,0:T(4,128)S(1)}, f32[20,4,68,2]{2,1,3,0:T(4,128)}, u32[]{:S(2)}, u32[]{:S(2)}) collective-permute-start(f32[20,4,68,2]{2,1,3,0:T(4,128)S(1)} %copy.225), channel_id=1, source_target_pairs={{0,4},{4,8},{8,12},{1,5},{5,9},{9,13},{2,6},{6,10},{10,14},{3,7},{... | collective-permute-start | bytes 130568 | tf_op jit(solution)/shard_map/ppermute | solution.py:22
  189.9 6.6 collective-permute-start.15
  209.9 2.6 collective-permute-start.16
  211.2 3.3 collective-permute-start.17
  216.9 8.2 %collective-permute-start.18 = (f32[20,4,24,4]{2,3,1,0:T(4,128)}, f32[20,4,24,4]{2,3,1,0:T(4,128)S(1)}, u32[]{:S(2)}, u32[]{:S(2)}) collective-permute-start(f32[20,4,24,4]{2,3,1,0:T(4,128)} %copy.126), channel_id=1, source_target_pairs={{0,4},{4,8},{8,12},{1,5},{5,9},{9,13},{2,6},{6,10},{10,14},{3,7},{... | collective-permute-start | bytes 92168 | tf_op jit(solution)/shard_map/ppermute | solution.py:22
  221.6 9.2 %collective-permute-start.19 = (f32[20,4,24,4]{2,3,1,0:T(4,128)S(1)}, f32[20,4,24,4]{2,3,1,0:T(4,128)}, u32[]{:S(2)}, u32[]{:S(2)}) collective-permute-start(f32[20,4,24,4]{2,3,1,0:T(4,128)S(1)} %copy.127), channel_id=1, source_target_pairs={{4,0},{8,4},{12,8},{5,1},{9,5},{13,9},{6,2},{10,6},{14,10},{7,3},{... | collective-permute-start | bytes 92168 | tf_op jit(solution)/shard_map/ppermute | solution.py:24
  279.5 2.6 collective-permute-start.20
  280.8 3.5 collective-permute-start.21
  288.7 9.1 %collective-permute-start.22 = (f32[20,4,26,5]{2,1,3,0:T(4,128)}, f32[20,4,26,5]{2,1,3,0:T(4,128)}, u32[]{:S(2)}, u32[]{:S(2)}) collective-permute-start(f32[20,4,26,5]{2,1,3,0:T(4,128)} %copy.130), channel_id=1, source_target_pairs={{0,4},{4,8},{8,12},{1,5},{5,9},{9,13},{2,6},{6,10},{10,14},{3,7},{... | collective-permute-start | bytes 124808 | tf_op jit(solution)/shard_map/ppermute | solution.py:22
  294.9 9.5 %collective-permute-start.23 = (f32[20,4,26,5]{2,1,3,0:T(4,128)}, f32[20,4,26,5]{2,1,3,0:T(4,128)}, u32[]{:S(2)}, u32[]{:S(2)}) collective-permute-start(f32[20,4,26,5]{2,1,3,0:T(4,128)} %copy.131), channel_id=1, source_target_pairs={{4,0},{8,4},{12,8},{5,1},{9,5},{13,9},{6,2},{10,6},{14,10},{7,3},{... | collective-permute-start | bytes 124808 | tf_op jit(solution)/shard_map/ppermute | solution.py:24
  319.0 245.7 %all-gather.11.cloned.1.call-start = ((), (), s32[]{:S(2)}) async-start(), calls=%async_computation.2 | async-start | bytes 2621440 | tf_op jit(solution)/shard_map/all_gather | solution.py:106
  372.2 2.9 collective-permute-start.24
  373.7 3.2 collective-permute-start.25
  383.9 12.1 %collective-permute-start.26 = (f32[20,4,68,2]{2,1,3,0:T(4,128)S(1)}, f32[20,4,68,2]{2,1,3,0:T(4,128)}, u32[]{:S(2)}, u32[]{:S(2)}) collective-permute-start(f32[20,4,68,2]{2,1,3,0:T(4,128)S(1)} %copy.227), channel_id=1, source_target_pairs={{0,4},{4,8},{8,12},{1,5},{5,9},{9,13},{2,6},{6,10},{10,14},{3,7},{... | collective-permute-start | bytes 130568 | tf_op jit(solution)/shard_map/ppermute | solution.py:22
  390.9 6.6 collective-permute-start.27
  410.9 2.6 collective-permute-start.28
  412.2 3.3 collective-permute-start.29
  417.9 8.2 %collective-permute-start.30 = (f32[20,4,24,4]{2,3,1,0:T(4,128)}, f32[20,4,24,4]{2,3,1,0:T(4,128)S(1)}, u32[]{:S(2)}, u32[]{:S(2)}) collective-permute-start(f32[20,4,24,4]{2,3,1,0:T(4,128)} %copy.141), channel_id=1, source_target_pairs={{0,4},{4,8},{8,12},{1,5},{5,9},{9,13},{2,6},{6,10},{10,14},{3,7},{... | collective-permute-start | bytes 92168 | tf_op jit(solution)/shard_map/ppermute | solution.py:22
  422.6 9.2 %collective-permute-start.31 = (f32[20,4,24,4]{2,3,1,0:T(4,128)S(1)}, f32[20,4,24,4]{2,3,1,0:T(4,128)}, u32[]{:S(2)}, u32[]{:S(2)}) collective-permute-start(f32[20,4,24,4]{2,3,1,0:T(4,128)S(1)} %copy.142), channel_id=1, source_target_pairs={{4,0},{8,4},{12,8},{5,1},{9,5},{13,9},{6,2},{10,6},{14,10},{7,3},{... | collective-permute-start | bytes 92168 | tf_op jit(solution)/shard_map/ppermute | solution.py:24
  480.4 2.6 collective-permute-start.32
  481.7 3.5 collective-permute-start.33
  489.6 9.1 %collective-permute-start.34 = (f32[20,4,26,5]{2,1,3,0:T(4,128)}, f32[20,4,26,5]{2,1,3,0:T(4,128)}, u32[]{:S(2)}, u32[]{:S(2)}) collective-permute-start(f32[20,4,26,5]{2,1,3,0:T(4,128)} %copy.145), channel_id=1, source_target_pairs={{0,4},{4,8},{8,12},{1,5},{5,9},{9,13},{2,6},{6,10},{10,14},{3,7},{... | collective-permute-start | bytes 124808 | tf_op jit(solution)/shard_map/ppermute | solution.py:22
  495.7 9.5 %collective-permute-start.35 = (f32[20,4,26,5]{2,1,3,0:T(4,128)}, f32[20,4,26,5]{2,1,3,0:T(4,128)}, u32[]{:S(2)}, u32[]{:S(2)}) collective-permute-start(f32[20,4,26,5]{2,1,3,0:T(4,128)} %copy.146), channel_id=1, source_target_pairs={{4,0},{8,4},{12,8},{5,1},{9,5},{13,9},{6,2},{10,6},{14,10},{7,3},{... | collective-permute-start | bytes 124808 | tf_op jit(solution)/shard_map/ppermute | solution.py:24
  573.3 2.9 collective-permute-start.36
  574.8 3.2 collective-permute-start.37
  585.0 12.0 %collective-permute-start.38 = (f32[20,4,68,2]{2,1,3,0:T(4,128)S(1)}, f32[20,4,68,2]{2,1,3,0:T(4,128)}, u32[]{:S(2)}, u32[]{:S(2)}) collective-permute-start(f32[20,4,68,2]{2,1,3,0:T(4,128)S(1)} %copy.229), channel_id=1, source_target_pairs={{0,4},{4,8},{8,12},{1,5},{5,9},{9,13},{2,6},{6,10},{10,14},{3,7},{... | collective-permute-start | bytes 130568 | tf_op jit(solution)/shard_map/ppermute | solution.py:22
  592.1 6.6 collective-permute-start.39
  612.0 2.6 collective-permute-start.40
  613.3 3.3 collective-permute-start.41
  619.0 8.0 %collective-permute-start.42 = (f32[20,4,24,4]{2,3,1,0:T(4,128)}, f32[20,4,24,4]{2,3,1,0:T(4,128)S(1)}, u32[]{:S(2)}, u32[]{:S(2)}) collective-permute-start(f32[20,4,24,4]{2,3,1,0:T(4,128)} %copy.156), channel_id=1, source_target_pairs={{0,4},{4,8},{8,12},{1,5},{5,9},{9,13},{2,6},{6,10},{10,14},{3,7},{... | collective-permute-start | bytes 92168 | tf_op jit(solution)/shard_map/ppermute | solution.py:22
  623.7 9.0 %collective-permute-start.43 = (f32[20,4,24,4]{2,3,1,0:T(4,128)S(1)}, f32[20,4,24,4]{2,3,1,0:T(4,128)}, u32[]{:S(2)}, u32[]{:S(2)}) collective-permute-start(f32[20,4,24,4]{2,3,1,0:T(4,128)S(1)} %copy.157), channel_id=1, source_target_pairs={{4,0},{8,4},{12,8},{5,1},{9,5},{13,9},{6,2},{10,6},{14,10},{7,3},{... | collective-permute-start | bytes 92168 | tf_op jit(solution)/shard_map/ppermute | solution.py:24
  (64 other events, 733.3 us)
Sparse Core Ops, SparseCore 0:
  117.7 45.0 all-gather.6
  319.2 44.5 all-gather.8
  520.1 44.5 all-gather.10
